TPU v7x, 32 devices: a whole 2x2x4 slice. The times are simulated.
32 devices in a mesh: dev: 32 (over z, y, x, core).
Axes of the slice: x: 2, y: 2, z: 4, core: 2. Of those that a mesh axis runs over, the one named last changes fastest.
Arguments:
- images: bfloat16 [256, 768, 1536], P('dev'), may hold values from -6 to 6
- legendre: bfloat16 [32, 704, 768], P('dev'), may hold values from -0.21875 to 0.21875
- leakage: float32 [32, 3, 13, 704], P('dev'), may hold values from -1 to 1
Outputs:
- modes: float32 [32, 704, 512], P('dev')
All inputs are finite; a program needn't handle non-finite values.
Results may differ from a plain program's by a relative error of at most 0.0053.
Values may be sent and summed in bfloat16 or wider, within the bound.
A program may use at most 128 MiB of HBM per device.

v0:
```python
import math
import jax
import jax.numpy as jnp
from jax import lax
from jax.sharding import PartitionSpec as P

BLK = 64
BAND = 6


def padded_2(cells, sides, width):
    for axis, dim in sides:
        count = lax.axis_size(axis)
        ends = count - 1
        head = lax.slice_in_dim(cells, 0, width, axis=dim)
        tail = lax.slice_in_dim(cells, cells.shape[dim] - width, cells.shape[dim], axis=dim)
        cells = jnp.concatenate(
            [
                lax.ppermute(tail, axis, [(i, (i + 1) % count) for i in range(ends)]),
                cells,
                lax.ppermute(head, axis, [((i + 1) % count, i) for i in range(ends)]),
            ],
            axis=dim,
        )
    return cells


def lon_table(nlon, norders):
    index = jnp.arange(nlon, dtype=jnp.int32)[None, :]
    order = jnp.arange(norders, dtype=jnp.int32)[:, None]
    phase = (index * order % nlon).astype(jnp.float32)
    angle = 2.0 * math.pi * phase / nlon
    table = jnp.stack([jnp.cos(angle), -jnp.sin(angle)], axis=1) / math.sqrt(nlon)
    return table.reshape(2 * norders, nlon).astype(jnp.bfloat16)


def time_table(ntimes):
    index = jnp.arange(ntimes, dtype=jnp.int32)
    phase = (index[:, None] * index[None, :] % ntimes).astype(jnp.float32)
    angle = 2.0 * math.pi * phase / ntimes
    cosine = jnp.cos(angle)
    sine = jnp.sin(angle)
    upper = jnp.concatenate([cosine, -sine], axis=1)
    lower = jnp.concatenate([sine, cosine], axis=1)
    return (jnp.concatenate([upper, lower], axis=0) / math.sqrt(ntimes)).astype(jnp.bfloat16)


def transform_images(table, block):
    out = jnp.einsum("kn,tan->kta", table, block, preferred_element_type=jnp.float32)
    return out.astype(jnp.bfloat16)


def on_device(images, legendre, leakage):
    devices = lax.axis_size("dev")
    here = lax.axis_index("dev")
    t_local, nlat, nlon = images.shape
    m_local, degrees_all, _ = legendre.shape
    norders = m_local * devices
    ntimes = t_local * devices
    table = lon_table(nlon, norders)
    whole = transform_images(table, images).reshape(norders, 2, t_local, nlat)
    gathered = lax.all_to_all(whole, "dev", split_axis=0, concat_axis=2, tiled=True)
    wtable = time_table(ntimes)
    nblocks = degrees_all // BLK
    local = 0
    order = here * m_local + local
    flat = gathered[local].reshape(2 * ntimes, nlat)
    rows_table = legendre[local]

    def one_block(block, spectra, order=order, flat=flat, rows_table=rows_table):
        start = block * BLK
        rows = lax.dynamic_slice_in_dim(rows_table, start, BLK, 0)
        coef = lax.dot_general(
            rows, flat, (((1,), (1,)), ((), ())), preferred_element_type=jnp.float32
        )
        degree = start + jnp.arange(BLK, dtype=jnp.int32)
        coef = jnp.where((degree >= order)[:, None], coef, jnp.float32(0.0)).astype(jnp.bfloat16)
        result = jnp.dot(coef, wtable, preferred_element_type=jnp.float32)
        return lax.dynamic_update_slice_in_dim(spectra, result, start, 0)

    first = order // BLK
    empty = jnp.zeros((degrees_all, 2 * ntimes), jnp.float32)
    spectra_list = [lax.fori_loop(first, jnp.int32(nblocks), one_block, empty)]
    spectra = jnp.stack(spectra_list, axis=0)
    padded = padded_2(spectra, (("dev", 0),), 1)
    padded = jnp.pad(padded, ((0, 0), (BAND, BAND), (0, 0)))
    degrees = jnp.arange(degrees_all, dtype=jnp.int32)
    local = 0
    order = here * m_local + local
    coeffs = leakage[local]
    total = jnp.zeros((degrees_all, 2 * ntimes), jnp.float32)
    for shift in range(3):
        for offset in range(2 * BAND + 1):
            total = (
                total
                + coeffs[shift, offset][:, None]
                * padded[local + shift, offset : offset + degrees_all]
            )
    outputs = [jnp.where((degrees >= order)[:, None], total, jnp.float32(0.0))]
    return jnp.stack(outputs, axis=0)


def solution(mesh):
    placed = (P("dev", None, None), P("dev", None, None), P("dev", None, None, None))
    return jax.shard_map(
        on_device, mesh=mesh, in_specs=placed, out_specs=P("dev", None, None), check_vma=False
    )
```

profile of v0, /device:TPU:1, one launch (start us, length us, event | category | flops | bytes accessed | tf_op | source)
XLA Modules:
  0.0 104.0 jit_solution(8679333870553698052)
XLA Ops:
  0.0 0.8 sine_negate_fusion
  1.2 12.1 %convolution_convert_fusion = bf16[64,8,768]{2,0,1:T(8,128)(2,1)S(1)} fusion(bf16[64,1536,1]{1,0,2:T(8,128)(2,1)S(1)} %reshape.393, bf16[8,768,1536]{2,1,0:T(8,128)(2,1)} %param.5), kind=kOutput, calls=%fused_computation.89 | convolution fusion | flops 1208352768 | bytes 19857408 | tf_op jit(solution)/shard_map/kn,tan->kta/dot_general | solution.py:49
  13.6 1.4 %copy.11 = bf16[32,2,8,768]{3,1,2,0:T(2,128)(2,1)} copy(bf16[32,2,8,768]{3,1,0,2:T(2,128)(2,1)S(1)} %reshape.392) | data formatting | bytes 1572864 | tf_op jit(solution)/shard_map/reshape | solution.py:61
  15.0 7.1 %all-to-all-start = ((bf16[32,2,8,768]{3,1,2,0:T(2,128)(2,1)}), bf16[32,2,8,768]{3,1,2,0:T(2,128)(2,1)S(1)}, u32[]{:S(2)}, u32[]{:S(2)}) async-start(bf16[32,2,8,768]{3,1,2,0:T(2,128)(2,1)} %copy.11), calls=%async_computation | async-start | bytes 1572864 | tf_op jit(solution)/shard_map/all_to_all | solution.py:62
  22.1 1.0 fusion.64
  23.1 1.0 fusion.62
  24.2 18.1 %all-to-all-done = bf16[32,2,8,768]{3,1,2,0:T(2,128)(2,1)S(1)} async-done(((bf16[32,2,8,768]{3,1,2,0:T(2,128)(2,1)}), bf16[32,2,8,768]{3,1,2,0:T(2,128)(2,1)S(1)}, u32[]{:S(2)}, u32[]{:S(2)}) %all-to-all-start) | async-done | bytes 786464 | tf_op jit(solution)/shard_map/all_to_all | solution.py:62
  42.6 16.0 %while.10 = (s32[]{:T(128)}, f32[704,512]{1,0:T(8,128)S(1)}, s32[]{:T(128)}, bf16[704,768]{1,0:T(8,128)(2,1)}, bf16[512,768]{1,0:T(8,128)(2,1)S(1)}, /*index=5*/...) while((s32[]{:T(128)}, f32[704,512]{1,0:T(8,128)S(1)}, s32[]{:T(128)}, ...), condition=%wide.region_1.2_spmd, body=%wide.region_0.1_spmd.sunk | while | flops 83951752 | bytes 1541851 | solution.py:83
  42.6 1.4 %convolution_dynamic-update-slice_fusion.2 = f32[704,512]{1,0:T(8,128)S(1)} fusion(f32[704,512]{1,0:T(8,128)S(1)} %get-tuple-element.140, s32[]{:T(128)S(6)} %select_n.82, bf16[512,512]{1,0:T(8,128)(2,1)S(1)} %get-tuple-element.154, bf16[512,768]{1,0:T(8,128)(2,1)S(1)} %get-tuple-element.153, bf16[704,768]{1,0:T(8,128)(2,1)} %get-tuple-element.152, ...), kind=kOutput, calls=%fused_computation.clone.1 | convolution fusion | flops 83951616 | bytes 1541632 | tf_op jit(solution)/shard_map/while/body/dot_general | solution.py:78
  44.1 1.4 %convolution_dynamic-update-slice_fusion.2 = f32[704,512]{1,0:T(8,128)S(1)} fusion(f32[704,512]{1,0:T(8,128)S(1)} %get-tuple-element.140, s32[]{:T(128)S(6)} %select_n.82, bf16[512,512]{1,0:T(8,128)(2,1)S(1)} %get-tuple-element.154, bf16[512,768]{1,0:T(8,128)(2,1)S(1)} %get-tuple-element.153, bf16[704,768]{1,0:T(8,128)(2,1)} %get-tuple-element.152, ...), kind=kOutput, calls=%fused_computation.clone.1 | convolution fusion | flops 83951616 | bytes 1541632 | tf_op jit(solution)/shard_map/while/body/dot_general | solution.py:78
  45.5 1.4 %convolution_dynamic-update-slice_fusion.2 = f32[704,512]{1,0:T(8,128)S(1)} fusion(f32[704,512]{1,0:T(8,128)S(1)} %get-tuple-element.140, s32[]{:T(128)S(6)} %select_n.82, bf16[512,512]{1,0:T(8,128)(2,1)S(1)} %get-tuple-element.154, bf16[512,768]{1,0:T(8,128)(2,1)S(1)} %get-tuple-element.153, bf16[704,768]{1,0:T(8,128)(2,1)} %get-tuple-element.152, ...), kind=kOutput, calls=%fused_computation.clone.1 | convolution fusion | flops 83951616 | bytes 1541632 | tf_op jit(solution)/shard_map/while/body/dot_general | solution.py:78
  47.0 1.4 %convolution_dynamic-update-slice_fusion.2 = f32[704,512]{1,0:T(8,128)S(1)} fusion(f32[704,512]{1,0:T(8,128)S(1)} %get-tuple-element.140, s32[]{:T(128)S(6)} %select_n.82, bf16[512,512]{1,0:T(8,128)(2,1)S(1)} %get-tuple-element.154, bf16[512,768]{1,0:T(8,128)(2,1)S(1)} %get-tuple-element.153, bf16[704,768]{1,0:T(8,128)(2,1)} %get-tuple-element.152, ...), kind=kOutput, calls=%fused_computation.clone.1 | convolution fusion | flops 83951616 | bytes 1541632 | tf_op jit(solution)/shard_map/while/body/dot_general | solution.py:78
  48.4 1.4 %convolution_dynamic-update-slice_fusion.2 = f32[704,512]{1,0:T(8,128)S(1)} fusion(f32[704,512]{1,0:T(8,128)S(1)} %get-tuple-element.140, s32[]{:T(128)S(6)} %select_n.82, bf16[512,512]{1,0:T(8,128)(2,1)S(1)} %get-tuple-element.154, bf16[512,768]{1,0:T(8,128)(2,1)S(1)} %get-tuple-element.153, bf16[704,768]{1,0:T(8,128)(2,1)} %get-tuple-element.152, ...), kind=kOutput, calls=%fused_computation.clone.1 | convolution fusion | flops 83951616 | bytes 1541632 | tf_op jit(solution)/shard_map/while/body/dot_general | solution.py:78
  49.9 1.4 %convolution_dynamic-update-slice_fusion.2 = f32[704,512]{1,0:T(8,128)S(1)} fusion(f32[704,512]{1,0:T(8,128)S(1)} %get-tuple-element.140, s32[]{:T(128)S(6)} %select_n.82, bf16[512,512]{1,0:T(8,128)(2,1)S(1)} %get-tuple-element.154, bf16[512,768]{1,0:T(8,128)(2,1)S(1)} %get-tuple-element.153, bf16[704,768]{1,0:T(8,128)(2,1)} %get-tuple-element.152, ...), kind=kOutput, calls=%fused_computation.clone.1 | convolution fusion | flops 83951616 | bytes 1541632 | tf_op jit(solution)/shard_map/while/body/dot_general | solution.py:78
  51.3 1.4 %convolution_dynamic-update-slice_fusion.2 = f32[704,512]{1,0:T(8,128)S(1)} fusion(f32[704,512]{1,0:T(8,128)S(1)} %get-tuple-element.140, s32[]{:T(128)S(6)} %select_n.82, bf16[512,512]{1,0:T(8,128)(2,1)S(1)} %get-tuple-element.154, bf16[512,768]{1,0:T(8,128)(2,1)S(1)} %get-tuple-element.153, bf16[704,768]{1,0:T(8,128)(2,1)} %get-tuple-element.152, ...), kind=kOutput, calls=%fused_computation.clone.1 | convolution fusion | flops 83951616 | bytes 1541632 | tf_op jit(solution)/shard_map/while/body/dot_general | solution.py:78
  52.8 1.4 %convolution_dynamic-update-slice_fusion.2 = f32[704,512]{1,0:T(8,128)S(1)} fusion(f32[704,512]{1,0:T(8,128)S(1)} %get-tuple-element.140, s32[]{:T(128)S(6)} %select_n.82, bf16[512,512]{1,0:T(8,128)(2,1)S(1)} %get-tuple-element.154, bf16[512,768]{1,0:T(8,128)(2,1)S(1)} %get-tuple-element.153, bf16[704,768]{1,0:T(8,128)(2,1)} %get-tuple-element.152, ...), kind=kOutput, calls=%fused_computation.clone.1 | convolution fusion | flops 83951616 | bytes 1541632 | tf_op jit(solution)/shard_map/while/body/dot_general | solution.py:78
  54.2 1.4 %convolution_dynamic-update-slice_fusion.2 = f32[704,512]{1,0:T(8,128)S(1)} fusion(f32[704,512]{1,0:T(8,128)S(1)} %get-tuple-element.140, s32[]{:T(128)S(6)} %select_n.82, bf16[512,512]{1,0:T(8,128)(2,1)S(1)} %get-tuple-element.154, bf16[512,768]{1,0:T(8,128)(2,1)S(1)} %get-tuple-element.153, bf16[704,768]{1,0:T(8,128)(2,1)} %get-tuple-element.152, ...), kind=kOutput, calls=%fused_computation.clone.1 | convolution fusion | flops 83951616 | bytes 1541632 | tf_op jit(solution)/shard_map/while/body/dot_general | solution.py:78
  55.7 1.4 %convolution_dynamic-update-slice_fusion.2 = f32[704,512]{1,0:T(8,128)S(1)} fusion(f32[704,512]{1,0:T(8,128)S(1)} %get-tuple-element.140, s32[]{:T(128)S(6)} %select_n.82, bf16[512,512]{1,0:T(8,128)(2,1)S(1)} %get-tuple-element.154, bf16[512,768]{1,0:T(8,128)(2,1)S(1)} %get-tuple-element.153, bf16[704,768]{1,0:T(8,128)(2,1)} %get-tuple-element.152, ...), kind=kOutput, calls=%fused_computation.clone.1 | convolution fusion | flops 83951616 | bytes 1541632 | tf_op jit(solution)/shard_map/while/body/dot_general | solution.py:78
  57.1 1.4 %convolution_dynamic-update-slice_fusion.2 = f32[704,512]{1,0:T(8,128)S(1)} fusion(f32[704,512]{1,0:T(8,128)S(1)} %get-tuple-element.140, s32[]{:T(128)S(6)} %select_n.82, bf16[512,512]{1,0:T(8,128)(2,1)S(1)} %get-tuple-element.154, bf16[512,768]{1,0:T(8,128)(2,1)S(1)} %get-tuple-element.153, bf16[704,768]{1,0:T(8,128)(2,1)} %get-tuple-element.152, ...), kind=kOutput, calls=%fused_computation.clone.1 | convolution fusion | flops 83951616 | bytes 1541632 | tf_op jit(solution)/shard_map/while/body/dot_general | solution.py:78
  58.6 2.5 %collective-permute-start.1 = (f32[1,704,512]{2,1,0:T(8,128)S(1)}, f32[1,704,512]{2,1,0:T(8,128)S(1)}, u32[]{:S(2)}, u32[]{:S(2)}) collective-permute-start(f32[1,704,512]{2,1,0:T(8,128)S(1)} %bitcast.23), channel_id=1, source_target_pairs={{1,0},{2,1},{3,2},{4,3},{5,4},{6,5},{7,6},{8,7},{9,8},{10,9},{11,1... | collective-permute-start | bytes 4325384 | tf_op jit(solution)/shard_map/ppermute | solution.py:21
  61.1 3.0 %collective-permute-start = (f32[1,704,512]{2,1,0:T(8,128)S(1)}, f32[1,704,512]{2,1,0:T(8,128)S(1)}, u32[]{:S(2)}, u32[]{:S(2)}) collective-permute-start(f32[1,704,512]{2,1,0:T(8,128)S(1)} %bitcast.24), channel_id=1, source_target_pairs={{0,1},{1,2},{2,3},{3,4},{4,5},{5,6},{6,7},{7,8},{8,9},{9,10},{10,1... | collective-permute-start | bytes 4325384 | tf_op jit(solution)/shard_map/ppermute | solution.py:19
  64.5 25.7 %collective-permute-done.1 = f32[1,704,512]{2,1,0:T(8,128)S(1)} collective-permute-done((f32[1,704,512]{2,1,0:T(8,128)S(1)}, f32[1,704,512]{2,1,0:T(8,128)S(1)}, u32[]{:S(2)}, u32[]{:S(2)}) %collective-permute-start.1) | collective-permute-done | bytes 1441824 | tf_op jit(solution)/shard_map/ppermute | solution.py:21
  90.3 4.8 %collective-permute-done = f32[1,704,512]{2,1,0:T(8,128)S(1)} collective-permute-done((f32[1,704,512]{2,1,0:T(8,128)S(1)}, f32[1,704,512]{2,1,0:T(8,128)S(1)}, u32[]{:S(2)}, u32[]{:S(2)}) %collective-permute-start) | collective-permute-done | bytes 1441824 | tf_op jit(solution)/shard_map/ppermute | solution.py:19
  95.7 8.4 %fusion.10 = f32[1,704,512]{2,1,0:T(8,128)} fusion(f32[3,716,512]{2,1,0:T(8,128)S(1)} %select_maximum_fusion, f32[1,704,512]{2,1,0:T(8,128)S(1)} %collective-permute-done.1, f32[704,512]{1,0:T(8,128)S(1)} %get-tuple-element.37, f32[1,704,512]{2,1,0:T(8,128)S(1)} %collective-permute-done, f32[704]{0:T(1024)S(1)} %get-tuple-element.39, ...), kind=kLoop, calls=%fused_computation.16 | loop fusion | flops 28114944 | bytes 57782208 | tf_op jit(solution)/shard_map/jit(_where)/select_n | solution.py:99
  (26 shorter events, 1.9 us)
Async XLA Ops:
  15.0 27.3 %all-to-all-start = ((bf16[32,2,8,768]{3,1,2,0:T(2,128)(2,1)}), bf16[32,2,8,768]{3,1,2,0:T(2,128)(2,1)S(1)}, u32[]{:S(2)}, u32[]{:S(2)}) async-start(bf16[32,2,8,768]{3,1,2,0:T(2,128)(2,1)} %copy.11), calls=%async_computation | async-start | bytes 1572864 | tf_op jit(solution)/shard_map/all_to_all | solution.py:62
  42.6 21.6 %copy-start = (f32[1,3,13,704]{3,0,2,1:T(1,128)S(1)}, f32[1,3,13,704]{3,0,2,1:T(1,128)}, u32[]{:S(2)}) copy-start(f32[1,3,13,704]{3,0,2,1:T(1,128)} %param.7) | copy-start | bytes 329476
  58.6 31.7 %collective-permute-start.1 = (f32[1,704,512]{2,1,0:T(8,128)S(1)}, f32[1,704,512]{2,1,0:T(8,128)S(1)}, u32[]{:S(2)}, u32[]{:S(2)}) collective-permute-start(f32[1,704,512]{2,1,0:T(8,128)S(1)} %bitcast.23), channel_id=1, source_target_pairs={{1,0},{2,1},{3,2},{4,3},{5,4},{6,5},{7,6},{8,7},{9,8},{10,9},{11,1... | collective-permute-start | bytes 4325384 | tf_op jit(solution)/shard_map/ppermute | solution.py:21
  61.1 34.0 %collective-permute-start = (f32[1,704,512]{2,1,0:T(8,128)S(1)}, f32[1,704,512]{2,1,0:T(8,128)S(1)}, u32[]{:S(2)}, u32[]{:S(2)}) collective-permute-start(f32[1,704,512]{2,1,0:T(8,128)S(1)} %bitcast.24), channel_id=1, source_target_pairs={{0,1},{1,2},{2,3},{3,4},{4,5},{5,6},{6,7},{7,8},{8,9},{9,10},{10,1... | collective-permute-start | bytes 4325384 | tf_op jit(solution)/shard_map/ppermute | solution.py:19
where the time goes:
time: 105 us; the launch traced here: 104 us
  waiting for transfers between devices  48.7 us (46%)
  matrix products  27.6 us (26%)
  starting transfers between devices  12.6 us (12%)
  other arithmetic  11.9 us (11%)
  local copies, waits for them, and re-layouts  2.61 us (2%)
    ppermute x1, waiting for transfers between devices, padded_2(): lax.ppermute(head, axis, [((i + 1) % count, i) for i in range(ends)])  25.7 us
    all_to_all x1, waiting for transfers between devices, on_device(): lax.all_to_all(whole, 'dev', split_axis=0, concat_axis=2, tiled=True)  18.1 us
    dot_general x11, matrix products, one_block(): result = jnp.dot(coef, wtable, preferred_element_type=jnp.float32)  15.5 us
    dot_general x1, matrix products, transform_images(): jnp.einsum('kn,tan->kta', table, block, preferred_element_type=jnp.float32)  12.1 us
    select_n x1, other arithmetic, on_device(): outputs = [jnp.where((degrees >= order)[:, None], total, jnp.float32(0.0))]  8.38 us
    all_to_all x1, starting transfers between devices, on_device(): lax.all_to_all(whole, 'dev', split_axis=0, concat_axis=2, tiled=True)  7.08 us
    ppermute x1, waiting for transfers between devices, padded_2(): lax.ppermute(tail, axis, [(i, (i + 1) % count) for i in range(ends)])  4.81 us
    ppermute x1, starting transfers between devices, padded_2(): lax.ppermute(tail, axis, [(i, (i + 1) % count) for i in range(ends)])  3.03 us
  transfers between devices with their start and end apart: 3, of which 3 were waited for; matrix products, arithmetic and copies ran while one was open for 2% of the time, Pallas kernels for 0%

commit v1 on v0

--- a/solution.py
+++ b/solution.py
@@ -59,7 +59,19 @@
     ntimes = t_local * devices
     table = lon_table(nlon, norders)
     whole = transform_images(table, images).reshape(norders, 2, t_local, nlat)
-    gathered = lax.all_to_all(whole, "dev", split_axis=0, concat_axis=2, tiled=True)
+
+    def resolve_the_words(vector, chip_axis):
+        return jnp.concatenate(
+            jax.lax.all_to_all(
+                jnp.stack(jnp.split(vector, jax.lax.axis_size(chip_axis), axis=0), axis=0),
+                axis_name=chip_axis,
+                concat_axis=0,
+                split_axis=0,
+            ),
+            axis=2,
+        )
+
+    gathered = resolve_the_words(whole, "dev")
     wtable = time_table(ntimes)
     nblocks = degrees_all // BLK
     local = 0

time: 105 us -> 123 us (1.17)
  local copies, waits for them, and re-layouts: 2.61 us -> 21.1 us
    unnamed x3 -> x34, local copies, waits for them, and re-layouts: 0.02 us -> 19.6 us
    reshape x2 -> x1, local copies, waits for them, and re-layouts: 1.72 us -> 0.08 us  [resolve_the_words(): jnp.concatenate(jax.lax.all_to_all(jnp.stack(jnp.split(vector, jax.lax.ax...]
where the time goes in v1:
time: 123 us
  waiting for transfers between devices  48.7 us (40%)
  matrix products  27.6 us (22%)
  local copies, waits for them, and re-layouts  21.1 us (17%)
  starting transfers between devices  12.6 us (10%)
  other arithmetic  11.9 us (10%)
    ppermute x1, waiting for transfers between devices, padded_2(): lax.ppermute(head, axis, [((i + 1) % count, i) for i in range(ends)])  25.7 us
    unnamed x34, local copies, waits for them, and re-layouts  19.6 us
    all_to_all x1, waiting for transfers between devices, resolve_the_words(): jax.lax.all_to_all(jnp.stack(jnp.split(vector, jax.lax.axis_size(chip_axi...  18.1 us
    dot_general x11, matrix products, one_block(): result = jnp.dot(coef, wtable, preferred_element_type=jnp.float32)  15.5 us
    dot_general x1, matrix products, transform_images(): jnp.einsum('kn,tan->kta', table, block, preferred_element_type=jnp.float32)  12.1 us
    select_n x1, other arithmetic, on_device(): outputs = [jnp.where((degrees >= order)[:, None], total, jnp.float32(0.0))]  8.38 us
    all_to_all x1, starting transfers between devices, resolve_the_words(): jax.lax.all_to_all(jnp.stack(jnp.split(vector, jax.lax.axis_size(chip_axi...  7.08 us
    ppermute x1, waiting for transfers between devices, padded_2(): lax.ppermute(tail, axis, [(i, (i + 1) % count) for i in range(ends)])  4.81 us
  transfers between devices with their start and end apart: 3, of which 3 were waited for; matrix products, arithmetic and copies ran while one was open for 2% of the time, Pallas kernels for 0%

profile of v1, /device:TPU:1, one launch (start us, length us, event | category | flops | bytes accessed | tf_op | source)
XLA Modules:
  0.0 122.6 jit_solution(4218115279579190836)
XLA Ops:
  0.0 0.8 sine_negate_fusion
  1.2 12.1 %convolution_convert_fusion = bf16[64,8,768]{2,0,1:T(8,128)(2,1)S(1)} fusion(bf16[64,1536,1]{1,0,2:T(8,128)(2,1)S(1)} %reshape.457, bf16[8,768,1536]{2,1,0:T(8,128)(2,1)} %param.5), kind=kOutput, calls=%fused_computation.89 | convolution fusion | flops 1208352768 | bytes 19857408 | tf_op jit(solution)/shard_map/kn,tan->kta/dot_general | solution.py:49
  13.9 0.6 constant_dynamic-update-slice_fusion.30
  33.6 7.1 %all-to-all-start = ((bf16[32,1,2,8,768]{4,2,3,1,0:T(2,128)(2,1)}), bf16[32,1,2,8,768]{4,2,3,1,0:T(2,128)(2,1)S(1)}, u32[]{:S(2)}, u32[]{:S(2)}) async-start(bf16[32,1,2,8,768]{4,2,3,1,0:T(2,128)(2,1)} %constant_dynamic-update-slice_fusion), calls=%async_computation | async-start | bytes 1572864 | tf_op jit(solution)/shard_map/all_to_all | solution.py:65
  40.7 1.0 fusion.64
  41.6 1.0 fusion.62
  42.7 18.1 %all-to-all-done = bf16[32,1,2,8,768]{4,2,3,1,0:T(2,128)(2,1)S(1)} async-done(((bf16[32,1,2,8,768]{4,2,3,1,0:T(2,128)(2,1)}), bf16[32,1,2,8,768]{4,2,3,1,0:T(2,128)(2,1)S(1)}, u32[]{:S(2)}, u32[]{:S(2)}) %all-to-all-start) | async-done | bytes 786464 | tf_op jit(solution)/shard_map/all_to_all | solution.py:65
  61.1 16.0 %while.10 = (s32[]{:T(128)}, f32[704,512]{1,0:T(8,128)S(1)}, s32[]{:T(128)}, bf16[704,768]{1,0:T(8,128)(2,1)}, bf16[512,768]{1,0:T(8,128)(2,1)S(1)}, /*index=5*/...) while((s32[]{:T(128)}, f32[704,512]{1,0:T(8,128)S(1)}, s32[]{:T(128)}, ...), condition=%wide.region_1.2_spmd, body=%wide.region_0.1_spmd.sunk | while | flops 83951752 | bytes 1541851 | solution.py:95
  61.2 1.4 %convolution_dynamic-update-slice_fusion.2 = f32[704,512]{1,0:T(8,128)S(1)} fusion(f32[704,512]{1,0:T(8,128)S(1)} %get-tuple-element.140, s32[]{:T(128)S(6)} %select_n.82, bf16[512,512]{1,0:T(8,128)(2,1)S(1)} %get-tuple-element.154, bf16[512,768]{1,0:T(8,128)(2,1)S(1)} %get-tuple-element.153, bf16[704,768]{1,0:T(8,128)(2,1)} %get-tuple-element.152, ...), kind=kOutput, calls=%fused_computation.clone.1 | convolution fusion | flops 83951616 | bytes 1541632 | tf_op jit(solution)/shard_map/while/body/dot_general | solution.py:90
  62.6 1.4 %convolution_dynamic-update-slice_fusion.2 = f32[704,512]{1,0:T(8,128)S(1)} fusion(f32[704,512]{1,0:T(8,128)S(1)} %get-tuple-element.140, s32[]{:T(128)S(6)} %select_n.82, bf16[512,512]{1,0:T(8,128)(2,1)S(1)} %get-tuple-element.154, bf16[512,768]{1,0:T(8,128)(2,1)S(1)} %get-tuple-element.153, bf16[704,768]{1,0:T(8,128)(2,1)} %get-tuple-element.152, ...), kind=kOutput, calls=%fused_computation.clone.1 | convolution fusion | flops 83951616 | bytes 1541632 | tf_op jit(solution)/shard_map/while/body/dot_general | solution.py:90
  64.1 1.4 %convolution_dynamic-update-slice_fusion.2 = f32[704,512]{1,0:T(8,128)S(1)} fusion(f32[704,512]{1,0:T(8,128)S(1)} %get-tuple-element.140, s32[]{:T(128)S(6)} %select_n.82, bf16[512,512]{1,0:T(8,128)(2,1)S(1)} %get-tuple-element.154, bf16[512,768]{1,0:T(8,128)(2,1)S(1)} %get-tuple-element.153, bf16[704,768]{1,0:T(8,128)(2,1)} %get-tuple-element.152, ...), kind=kOutput, calls=%fused_computation.clone.1 | convolution fusion | flops 83951616 | bytes 1541632 | tf_op jit(solution)/shard_map/while/body/dot_general | solution.py:90
  65.5 1.4 %convolution_dynamic-update-slice_fusion.2 = f32[704,512]{1,0:T(8,128)S(1)} fusion(f32[704,512]{1,0:T(8,128)S(1)} %get-tuple-element.140, s32[]{:T(128)S(6)} %select_n.82, bf16[512,512]{1,0:T(8,128)(2,1)S(1)} %get-tuple-element.154, bf16[512,768]{1,0:T(8,128)(2,1)S(1)} %get-tuple-element.153, bf16[704,768]{1,0:T(8,128)(2,1)} %get-tuple-element.152, ...), kind=kOutput, calls=%fused_computation.clone.1 | convolution fusion | flops 83951616 | bytes 1541632 | tf_op jit(solution)/shard_map/while/body/dot_general | solution.py:90
  67.0 1.4 %convolution_dynamic-update-slice_fusion.2 = f32[704,512]{1,0:T(8,128)S(1)} fusion(f32[704,512]{1,0:T(8,128)S(1)} %get-tuple-element.140, s32[]{:T(128)S(6)} %select_n.82, bf16[512,512]{1,0:T(8,128)(2,1)S(1)} %get-tuple-element.154, bf16[512,768]{1,0:T(8,128)(2,1)S(1)} %get-tuple-element.153, bf16[704,768]{1,0:T(8,128)(2,1)} %get-tuple-element.152, ...), kind=kOutput, calls=%fused_computation.clone.1 | convolution fusion | flops 83951616 | bytes 1541632 | tf_op jit(solution)/shard_map/while/body/dot_general | solution.py:90
  68.4 1.4 %convolution_dynamic-update-slice_fusion.2 = f32[704,512]{1,0:T(8,128)S(1)} fusion(f32[704,512]{1,0:T(8,128)S(1)} %get-tuple-element.140, s32[]{:T(128)S(6)} %select_n.82, bf16[512,512]{1,0:T(8,128)(2,1)S(1)} %get-tuple-element.154, bf16[512,768]{1,0:T(8,128)(2,1)S(1)} %get-tuple-element.153, bf16[704,768]{1,0:T(8,128)(2,1)} %get-tuple-element.152, ...), kind=kOutput, calls=%fused_computation.clone.1 | convolution fusion | flops 83951616 | bytes 1541632 | tf_op jit(solution)/shard_map/while/body/dot_general | solution.py:90
  69.9 1.4 %convolution_dynamic-update-slice_fusion.2 = f32[704,512]{1,0:T(8,128)S(1)} fusion(f32[704,512]{1,0:T(8,128)S(1)} %get-tuple-element.140, s32[]{:T(128)S(6)} %select_n.82, bf16[512,512]{1,0:T(8,128)(2,1)S(1)} %get-tuple-element.154, bf16[512,768]{1,0:T(8,128)(2,1)S(1)} %get-tuple-element.153, bf16[704,768]{1,0:T(8,128)(2,1)} %get-tuple-element.152, ...), kind=kOutput, calls=%fused_computation.clone.1 | convolution fusion | flops 83951616 | bytes 1541632 | tf_op jit(solution)/shard_map/while/body/dot_general | solution.py:90
  71.3 1.4 %convolution_dynamic-update-slice_fusion.2 = f32[704,512]{1,0:T(8,128)S(1)} fusion(f32[704,512]{1,0:T(8,128)S(1)} %get-tuple-element.140, s32[]{:T(128)S(6)} %select_n.82, bf16[512,512]{1,0:T(8,128)(2,1)S(1)} %get-tuple-element.154, bf16[512,768]{1,0:T(8,128)(2,1)S(1)} %get-tuple-element.153, bf16[704,768]{1,0:T(8,128)(2,1)} %get-tuple-element.152, ...), kind=kOutput, calls=%fused_computation.clone.1 | convolution fusion | flops 83951616 | bytes 1541632 | tf_op jit(solution)/shard_map/while/body/dot_general | solution.py:90
  72.8 1.4 %convolution_dynamic-update-slice_fusion.2 = f32[704,512]{1,0:T(8,128)S(1)} fusion(f32[704,512]{1,0:T(8,128)S(1)} %get-tuple-element.140, s32[]{:T(128)S(6)} %select_n.82, bf16[512,512]{1,0:T(8,128)(2,1)S(1)} %get-tuple-element.154, bf16[512,768]{1,0:T(8,128)(2,1)S(1)} %get-tuple-element.153, bf16[704,768]{1,0:T(8,128)(2,1)} %get-tuple-element.152, ...), kind=kOutput, calls=%fused_computation.clone.1 | convolution fusion | flops 83951616 | bytes 1541632 | tf_op jit(solution)/shard_map/while/body/dot_general | solution.py:90
  74.2 1.4 %convolution_dynamic-update-slice_fusion.2 = f32[704,512]{1,0:T(8,128)S(1)} fusion(f32[704,512]{1,0:T(8,128)S(1)} %get-tuple-element.140, s32[]{:T(128)S(6)} %select_n.82, bf16[512,512]{1,0:T(8,128)(2,1)S(1)} %get-tuple-element.154, bf16[512,768]{1,0:T(8,128)(2,1)S(1)} %get-tuple-element.153, bf16[704,768]{1,0:T(8,128)(2,1)} %get-tuple-element.152, ...), kind=kOutput, calls=%fused_computation.clone.1 | convolution fusion | flops 83951616 | bytes 1541632 | tf_op jit(solution)/shard_map/while/body/dot_general | solution.py:90
  75.7 1.4 %convolution_dynamic-update-slice_fusion.2 = f32[704,512]{1,0:T(8,128)S(1)} fusion(f32[704,512]{1,0:T(8,128)S(1)} %get-tuple-element.140, s32[]{:T(128)S(6)} %select_n.82, bf16[512,512]{1,0:T(8,128)(2,1)S(1)} %get-tuple-element.154, bf16[512,768]{1,0:T(8,128)(2,1)S(1)} %get-tuple-element.153, bf16[704,768]{1,0:T(8,128)(2,1)} %get-tuple-element.152, ...), kind=kOutput, calls=%fused_computation.clone.1 | convolution fusion | flops 83951616 | bytes 1541632 | tf_op jit(solution)/shard_map/while/body/dot_general | solution.py:90
  77.1 2.5 %collective-permute-start.1 = (f32[1,704,512]{2,1,0:T(8,128)S(1)}, f32[1,704,512]{2,1,0:T(8,128)S(1)}, u32[]{:S(2)}, u32[]{:S(2)}) collective-permute-start(f32[1,704,512]{2,1,0:T(8,128)S(1)} %bitcast.146), channel_id=1, source_target_pairs={{1,0},{2,1},{3,2},{4,3},{5,4},{6,5},{7,6},{8,7},{9,8},{10,9},{11,1... | collective-permute-start | bytes 4325384 | tf_op jit(solution)/shard_map/ppermute | solution.py:21
  79.7 3.0 %collective-permute-start = (f32[1,704,512]{2,1,0:T(8,128)S(1)}, f32[1,704,512]{2,1,0:T(8,128)S(1)}, u32[]{:S(2)}, u32[]{:S(2)}) collective-permute-start(f32[1,704,512]{2,1,0:T(8,128)S(1)} %bitcast.147), channel_id=1, source_target_pairs={{0,1},{1,2},{2,3},{3,4},{4,5},{5,6},{6,7},{7,8},{8,9},{9,10},{10,1... | collective-permute-start | bytes 4325384 | tf_op jit(solution)/shard_map/ppermute | solution.py:19
  83.1 25.7 %collective-permute-done.1 = f32[1,704,512]{2,1,0:T(8,128)S(1)} collective-permute-done((f32[1,704,512]{2,1,0:T(8,128)S(1)}, f32[1,704,512]{2,1,0:T(8,128)S(1)}, u32[]{:S(2)}, u32[]{:S(2)}) %collective-permute-start.1) | collective-permute-done | bytes 1441824 | tf_op jit(solution)/shard_map/ppermute | solution.py:21
  108.8 4.8 %collective-permute-done = f32[1,704,512]{2,1,0:T(8,128)S(1)} collective-permute-done((f32[1,704,512]{2,1,0:T(8,128)S(1)}, f32[1,704,512]{2,1,0:T(8,128)S(1)}, u32[]{:S(2)}, u32[]{:S(2)}) %collective-permute-start) | collective-permute-done | bytes 1441824 | tf_op jit(solution)/shard_map/ppermute | solution.py:19
  114.2 8.4 %fusion.10 = f32[1,704,512]{2,1,0:T(8,128)} fusion(f32[3,716,512]{2,1,0:T(8,128)S(1)} %select_maximum_fusion, f32[1,704,512]{2,1,0:T(8,128)S(1)} %collective-permute-done.1, f32[704,512]{1,0:T(8,128)S(1)} %get-tuple-element.37, f32[1,704,512]{2,1,0:T(8,128)S(1)} %collective-permute-done, f32[704]{0:T(1024)S(1)} %get-tuple-element.39, ...), kind=kLoop, calls=%fused_computation.16 | loop fusion | flops 28114944 | bytes 57782208 | tf_op jit(solution)/shard_map/jit(_where)/select_n | solution.py:111
  (56 shorter events, 21.2 us)
Async XLA Ops:
  33.6 27.3 %all-to-all-start = ((bf16[32,1,2,8,768]{4,2,3,1,0:T(2,128)(2,1)}), bf16[32,1,2,8,768]{4,2,3,1,0:T(2,128)(2,1)S(1)}, u32[]{:S(2)}, u32[]{:S(2)}) async-start(bf16[32,1,2,8,768]{4,2,3,1,0:T(2,128)(2,1)} %constant_dynamic-update-slice_fusion), calls=%async_computation | async-start | bytes 1572864 | tf_op jit(solution)/shard_map/all_to_all | solution.py:65
  61.1 21.6 %copy-start = (f32[1,3,13,704]{3,0,2,1:T(1,128)S(1)}, f32[1,3,13,704]{3,0,2,1:T(1,128)}, u32[]{:S(2)}) copy-start(f32[1,3,13,704]{3,0,2,1:T(1,128)} %param.7) | copy-start | bytes 329476
  77.1 31.7 %collective-permute-start.1 = (f32[1,704,512]{2,1,0:T(8,128)S(1)}, f32[1,704,512]{2,1,0:T(8,128)S(1)}, u32[]{:S(2)}, u32[]{:S(2)}) collective-permute-start(f32[1,704,512]{2,1,0:T(8,128)S(1)} %bitcast.146), channel_id=1, source_target_pairs={{1,0},{2,1},{3,2},{4,3},{5,4},{6,5},{7,6},{8,7},{9,8},{10,9},{11,1... | collective-permute-start | bytes 4325384 | tf_op jit(solution)/shard_map/ppermute | solution.py:21
  79.7 34.0 %collective-permute-start = (f32[1,704,512]{2,1,0:T(8,128)S(1)}, f32[1,704,512]{2,1,0:T(8,128)S(1)}, u32[]{:S(2)}, u32[]{:S(2)}) collective-permute-start(f32[1,704,512]{2,1,0:T(8,128)S(1)} %bitcast.147), channel_id=1, source_target_pairs={{0,1},{1,2},{2,3},{3,4},{4,5},{5,6},{6,7},{7,8},{8,9},{9,10},{10,1... | collective-permute-start | bytes 4325384 | tf_op jit(solution)/shard_map/ppermute | solution.py:19
